TPU v7x, 256 devices: a whole 4x4x8 slice. The times are simulated.
256 devices in a mesh: grp: 8 (over z), row: 32 (over y, x, core).
Axes of the slice: x: 4, y: 4, z: 8, core: 2. Of those that a mesh axis runs over, the one named last changes fastest.
Arguments:
- gradient: float32 [8, 4096, 1024], P('grp', 'row'), may hold values from -8000 to 8000
- weight: float32 [8, 4096, 1024], P('grp', 'row'), may hold values from -0.09375 to 0.09375
- dual: float32 [8, 1024, 1024], P('grp'), may hold values from -6 to 6
Outputs:
- update: float32 [8, 4096, 1024], P('grp', 'row')
- dual_next: float32 [8, 1024, 1024], P('grp', 'row')
All inputs are finite; a program needn't handle non-finite values.
Results may differ from a plain program's by a relative error of at most 0.03.
Values may be sent and summed in bfloat16 or wider, within the bound.
A program may use at most 64 MiB of HBM per device.

v0:
```python
import math

import jax
import jax.numpy as jnp
from jax import lax
from jax.experimental import pallas as pl
from jax.experimental.pallas import tpu as pltpu
from jax.sharding import Mesh
from jax.sharding import PartitionSpec as P

ROW = ("row_0", "row_1", "row_2")
MESH = pl.DeviceIdType.MESH
coef_a = 3.4445
coef_b = -4.775
coef_c = 2.0315
epsilon = 1e-06
WIN = 640
STEP_AT = (1, 6, 10, 14, 18, 22, 27)
F32 = jnp.float32
BF16 = jnp.bfloat16


class Copies:
    def __init__(self, send, recv):
        self.send, self.recv, self.n = send, recv, 0

    def __call__(self, src, dst, where):
        i = self.n
        self.n += 1
        copy = pltpu.make_async_remote_copy(
            src_ref=src, dst_ref=dst, send_sem=self.send.at[i], recv_sem=self.recv.at[i],
            device_id=where, device_id_type=MESH,
        )
        copy.start()
        return copy


def turn(p, d, n):
    return lax.rem(p + d, n)


class RingSum:
    def __init__(self, copies, axis, p, part, bufs, lo, hi):
        self.c, self.axis, self.p, self.part = copies, axis, p, part
        self.t, self.u, self.r = bufs
        self.lo, self.hi = lo, hi

    def first(self):
        c, p, part, t, r = self.c, self.p, self.part, self.t, self.r
        right, left, far = turn(p, 1, 4), turn(p, 3, 4), turn(p, 2, 4)
        to_r, to_l = {self.axis: right}, {self.axis: left}
        lo, hi = self.lo, self.hi
        self.a = c(part.at[(far, *lo)], t.at[0], to_r)
        self.b = c(part.at[(far, *hi)], t.at[1], to_l)
        self.e = c(part.at[(right, *hi)], r.at[(0, *hi)], to_r)
        self.f = c(part.at[(left, *lo)], r.at[(1, *lo)], to_l)

    def second(self):
        c, p, part, t, u, r = self.c, self.p, self.part, self.t, self.u, self.r
        right, left = turn(p, 1, 4), turn(p, 3, 4)
        lo, hi = self.lo, self.hi
        self.a.wait_recv()
        u[0] = (part[(right, *lo)].astype(F32) + t[0].astype(F32)).astype(u.dtype)
        self.g = c(u.at[0], r.at[(0, *lo)], {self.axis: right})
        self.b.wait_recv()
        u[1] = (part[(left, *hi)].astype(F32) + t[1].astype(F32)).astype(u.dtype)
        self.i = c(u.at[1], r.at[(1, *hi)], {self.axis: left})

    def third(self):
        for copy in (self.e, self.f, self.g, self.i):
            copy.wait_recv()
        return self.part[self.p].astype(F32) + self.r[0].astype(F32) + self.r[1].astype(F32)

    def drain(self):
        for copy in (self.a, self.b, self.e, self.f, self.g, self.i):
            copy.wait_send()


class RingSpread:
    def __init__(self, copies, axis, p, at, lo, hi):
        self.c, self.axis, self.p = copies, axis, p
        self.lo = lambda i: at(i, lo)
        self.hi = lambda i: at(i, hi)

    def first(self):
        c, p, lo, hi = self.c, self.p, self.lo, self.hi
        to_r, to_l = {self.axis: turn(p, 1, 4)}, {self.axis: turn(p, 3, 4)}
        self.a = c(lo(p), lo(p), to_r)
        self.b = c(hi(p), hi(p), to_l)
        self.e = c(hi(p), hi(p), to_r)
        self.f = c(lo(p), lo(p), to_l)

    def second(self):
        c, p, lo, hi = self.c, self.p, self.lo, self.hi
        right, left = turn(p, 1, 4), turn(p, 3, 4)
        self.a.wait_recv()
        self.g = c(lo(left), lo(left), {self.axis: right})
        self.b.wait_recv()
        self.i = c(hi(right), hi(right), {self.axis: left})

    def near(self):
        self.e.wait_recv()
        self.f.wait_recv()

    def last(self):
        self.g.wait_recv()
        self.i.wait_recv()

    def drain(self):
        for copy in (self.a, self.b, self.e, self.f, self.g, self.i):
            copy.wait_send()


def everywhere(c, x, y, k, parts_a, parts_b, bufs, cut1, cut2, near_at, far_at, order):
    other = {"row_2": 1 - k}
    ba, bb, qa, qb, ba2, bb2 = bufs
    dtype = qa.dtype
    near_a, near_b = near_at
    far_a_at, far_b_at = far_at
    sum_a = RingSum(c, "row_1", x, parts_a, ba, *cut1)
    sum_b = RingSum(c, "row_0", y, parts_b, bb, *cut1)
    sum_a.first()
    sum_b.first()
    yield
    sum_a.second()
    sum_b.second()
    yield
    va = sum_a.third().astype(dtype)
    for j in range(4):
        qa[j] = va[16 * j:16 * j + 16]
    sum_a2 = RingSum(c, "row_0", y, qa, ba2, *cut2)
    sum_a2.first()
    vb = sum_b.third().astype(dtype)
    for j in range(4):
        qb[j] = vb[16 * j:16 * j + 16]
    sum_b2 = RingSum(c, "row_1", x, qb, bb2, *cut2)
    sum_b2.first()
    yield
    sum_a2.second()
    sum_b2.second()
    yield
    near_a(y, ())[...] = sum_a2.third().astype(dtype)
    spread_a = RingSpread(c, "row_0", y, near_a, *cut2)
    spread_a.first()
    near_b(x, ())[...] = sum_b2.third().astype(dtype)
    spread_b = RingSpread(c, "row_1", x, near_b, *cut2)
    spread_b.first()
    yield
    spread_a.second()
    spread_b.second()
    yield
    spread_a.near()
    spread_a.last()
    halves = (pl.ds(0, 2), pl.ds(2, 2))
    far_a = RingSpread(c, "row_1", x, far_a_at, *halves)
    far_a.first()
    every = slice(None)
    pair = lambda ref: c(ref, ref, other)
    shared = [pair(far_a_at(x, every))]
    spread_b.near()
    spread_b.last()
    far_b = RingSpread(c, "row_0", y, far_b_at, *halves)
    far_b.first()
    shared += [pair(far_b_at(y, every))]
    yield
    far_a.second()
    far_b.second()
    yield
    far_a.near()
    shared += [pair(far_a_at(turn(x, d, 4), every)) for d in (1, 3)]
    far_b.near()
    shared += [pair(far_b_at(turn(y, d, 4), every)) for d in (1, 3)]
    yield
    far_a.last()
    shared += [pair(far_a_at(turn(x, 2, 4), every))]
    far_b.last()
    shared += [pair(far_b_at(turn(y, 2, 4), every))]
    yield
    for copy in shared:
        copy.wait_recv()
    order.append(shared)
    order.append((sum_a, sum_b, sum_a2, sum_b2, spread_a, spread_b, far_a, far_b))


def kernel(threshold, g_hbm, w_hbm, d_hbm, x_out, dual_out,
           g_ref, w_v, d_v, wst, wt, wt2, g2, stat_s, stat_r, xd, wd, cp, pa, pb, fin, gf, gh, p0, p1, p2, uf, ub,
           ca, cb, cfin, bufs_g, bufs_c, in_sem, send, recv):
    z = lax.axis_index("grp")
    y = lax.axis_index("row_0")
    x = lax.axis_index("row_1")
    k = lax.axis_index("row_2")
    other = 1 - k
    c = Copies(send, recv)
    load_d = pltpu.make_async_copy(d_hbm, d_v, in_sem.at[0])
    load_w = pltpu.make_async_copy(w_hbm, w_v, in_sem.at[1])
    load_g = pltpu.make_async_copy(g_hbm, g_ref, in_sem.at[2])
    load_g.start()
    load_w.start()
    load_d.start()

    barrier = pltpu.get_barrier_semaphore()
    partner = {"row_2": other}
    plane = [{"row_0": turn(y, e, 4), "row_1": turn(x, d, 4), "row_2": turn(k, f, 2)}
             for e in range(4) for d in range(4) for f in range(2) if (e, d, f) != (0, 0, 0)]
    line = [{"grp": turn(z, d, 8)} for d in range(1, 8)]
    for peer in plane + line:
        pl.semaphore_signal(barrier, inc=1, device_id=peer, device_id_type=MESH)

    load_g.wait()
    g = g_ref[...]
    total = jnp.full((1, 128), jnp.sum(g * g), F32)
    stat_s[0] = total
    own = pl.ds(pl.multiple_of(128 * k, 128), 128)
    theirs = pl.ds(pl.multiple_of(128 * other, 128), 128)
    pl.semaphore_wait(barrier, len(plane) + len(line))
    stats = [c(stat_s.at[0], stat_r.at[i], peer) for i, peer in enumerate(plane)]
    pairs = [c(g_ref, g2, partner)]
    load_w.wait()
    w = w_v[...]
    wh = w.astype(BF16)
    wst[0:128] = wh
    wst[128:256] = (w - wh.astype(F32)).astype(BF16)
    wd[own] = wh
    pairs.append(c(wd.at[own], wd.at[own], partner))
    load_d.wait()

    def split(v):
        vh = v.astype(BF16)
        return vh, (v - vh.astype(F32)).astype(BF16)

    def weighted_chunk(j):
        cols = pl.ds(256 * j, 256)
        dh, dl = split(d_v[:, cols])
        both = jnp.dot(wst[...], dh, preferred_element_type=F32)
        acc = both[:128] + both[128:] + jnp.dot(wst[0:128], dl, preferred_element_type=F32)
        dh, dl = split(d_v[cols, :])
        dims = (((1,), (1,)), ((), ()))
        both = lax.dot_general(wst[...], dh, dims, preferred_element_type=F32)
        acc += both[:128] + both[128:]
        acc += lax.dot_general(wst[0:128], dl, dims, preferred_element_type=F32)
        wt[:, cols] = 0.5 * acc

    def half_weighted(m):
        for n in (2 * m, 2 * m + 1):
            weighted_chunk(n)
        cols = pl.ds(512 * m, 512)
        pairs.append(c(wt.at[:, cols], wt2.at[:, cols], partner))

    half_weighted(0)
    for i, copy in enumerate(stats):
        copy.wait_recv()
        total += stat_r[i]
    stat_s[1] = total
    lines = [c(stat_s.at[1], stat_r.at[31 + i], peer) for i, peer in enumerate(line)]
    half_weighted(1)
    for copy in pairs:
        copy.wait_recv()
    for i, copy in enumerate(lines):
        copy.wait_recv()
        total += stat_r[31 + i]

    clip = jnp.minimum(1.0, threshold * lax.rsqrt(total[0:1, 0:1]))
    for rows, ga, wa in ((own, g_ref, wt), (theirs, g2, wt2)):
        t = (clip * ga[...] + wa[...]).astype(BF16)
        xd[rows, 0:1024] = t
        xd[rows, 1024:1536] = t[:, 0:512]

    tn = (((0,), (0,)), ((), ()))
    for i in range(4):
        at = pl.multiple_of(128 * (2 * i + k), 128)
        part = lax.dot_general(
            xd[:, pl.ds(at, 128)], xd[:, pl.ds(at, WIN)], tn, preferred_element_type=F32)
        pa[i] = part[:64]
        pb[i] = part[64:]

    ended = []
    rows8 = ((pl.ds(0, 8),), (pl.ds(8, 8),))
    rows32 = ((pl.ds(0, 32),), (pl.ds(32, 32),))
    gram_steps = everywhere(
        c, x, y, k, pa, pb, bufs_g, rows32, rows8,
        (lambda j, h: fin.at[(x, k, 0, j, *h)], lambda j, h: fin.at[(y, k, 1, j, *h)]),
        (lambda i, h: fin.at[i, k, 0, h], lambda i, h: fin.at[i, k, 1, h]), ended)
    next(gram_steps)
    next(gram_steps)
    for b in range(8):
        part = lax.dot_general(
            wd[:, 128 * b:128 * b + 128], xd[:, 0:1024], tn, preferred_element_type=F32)
        cp[b] = part.astype(BF16).reshape(2, 2, 2, 16, 1024)
    for e in range(4):
        for d in range(4):
            ca[d, 16 * e:16 * e + 16] = cp[2 * e + d // 2, d % 2, k, 0]
            cb[e, 16 * d:16 * d + 16] = cp[2 * e + d // 2, d % 2, k, 1]
    for _ in range(6):
        next(gram_steps)

    cols512 = ((slice(None), pl.ds(0, 512)), (slice(None), pl.ds(512, 512)))
    steps = everywhere(
        c, x, y, k, ca, cb, bufs_c, rows32, cols512,
        (lambda j, h: cfin.at[(j, x, k, 0, *h)], lambda j, h: cfin.at[(y, j, k, 1, *h)]),
        (lambda i, h: cfin.at[h, i, k, 0], lambda i, h: cfin.at[i, h, k, 1]), ended)
    next(steps)
    for _ in gram_steps:
        pass

    trace = jnp.zeros((1, 1), F32)
    eye = (lax.broadcasted_iota(jnp.int32, (128, 128), 0)
           == lax.broadcasted_iota(jnp.int32, (128, 128), 1))
    for b in range(8):
        i, core = b // 2, b % 2
        for j in range(5):
            m = (b + j) % 8
            block = fin[i, core, :, :, :, 128 * j:128 * j + 128].reshape(128, 128)
            rows, cols = pl.ds(128 * b, 128), pl.ds(128 * m, 128)
            gf[rows, cols] = block
            gh[rows, cols] = block.astype(BF16)
            if j == 0:
                trace += jnp.sum(jnp.where(eye, block, 0.0), keepdims=True)
            if 0 < j < 4:
                block = block.T
                gf[cols, rows] = block
                gh[cols, rows] = block.astype(BF16)
    scale = 1.0 / (trace + epsilon)
    root = jnp.sqrt(scale)

    def dot(u, v):
        return jnp.dot(u, v, preferred_element_type=F32)

    TILE = 256
    tiles = [pl.ds(TILE * n, TILE) for n in range(1024 // TILE)]
    done = [0]

    def advance():
        done[0] += 1
        if done[0] in STEP_AT:
            next(steps, None)

    for step, p in enumerate((p0, p1, p2)):
        s = scale if step == 0 else 1.0
        for n in tiles:
            p[:, n] = ((coef_b * s) * gf[:, n]
                       + (coef_c * s * s) * dot(gh[...], gh[:, n])).astype(BF16)
            advance()
        if step < 2:
            for n in tiles:
                u = coef_a * gf[:, n] + dot(p[...], gh[:, n])
                uf[:, n] = u
                ub[:, n] = u.astype(BF16)
                advance()
            for n in tiles:
                v = s * (coef_a * uf[:, n] + dot(ub[...], p[:, n]))
                gf[:, n] = v
                gh[:, n] = v.astype(BF16)
                advance()

    mine = cfin[y, x, k].reshape(32, 1024)
    share = 8 * y + 2 * x + k
    unit = (lax.broadcasted_iota(jnp.int32, (32, 1024), 0) + 32 * share
            == lax.broadcasted_iota(jnp.int32, (32, 1024), 1))
    low = jnp.concatenate([xd[own, 0:1024], mine, unit.astype(F32).astype(BF16)], axis=0)
    v = coef_a * low.astype(F32) + dot(low, p0[...])
    v = coef_a * v + dot(v.astype(BF16), p1[...])
    v = coef_a * v + dot(v.astype(BF16), p2[...])

    def by_gram(v):
        v = dot((coef_a * v + dot(v.astype(BF16), p2[...])).astype(BF16), gh[...])
        return coef_a * v + dot(v.astype(BF16), p2[...])

    next(steps)
    once = by_gram(v)
    next(steps)
    v = coef_a * v + coef_b * once + coef_c * by_gram(once)
    for _ in steps:
        pass
    x_out[...] = (root * v[0:128]).astype(BF16)
    cross = v[128:160] + lax.dot_general(
        v[160:192].astype(BF16), cfin[...].reshape(1024, 1024), (((1,), (1,)), ((), ())),
        preferred_element_type=F32)
    dual_out[...] = d_v[pl.ds(pl.multiple_of(32 * share, 32), 32), :] - (16.0 * root) * cross

    for copy in stats + lines + pairs:
        copy.wait_send()
    for group in ended:
        for item in group:
            item.drain() if hasattr(item, "drain") else item.wait_send()


def step_of(gradient, weight, dual, threshold):
    vmem = lambda *s: pltpu.VMEM(s, F32)
    half = lambda *s: pltpu.VMEM(s, BF16)

    def bufs(kind, width, cut2):
        first = [kind(2, 32, width), kind(2, 32, width), kind(2, 64, width)]
        second = [kind(2, *cut2), kind(2, *cut2), kind(2, 16, width)]
        return [first, first, kind(4, 16, width), kind(4, 16, width), second, second]

    n_copies = 38 + 4 + 2 * (8 * 6 + 8)
    return pl.pallas_call(
        lambda *refs: kernel(threshold, *refs),
        out_shape=(jax.ShapeDtypeStruct((128, 1024), BF16),
                   jax.ShapeDtypeStruct((32, 1024), F32)),
        in_specs=[pl.BlockSpec(memory_space=pltpu.HBM)] * 3,
        out_specs=[pl.BlockSpec(memory_space=pltpu.VMEM)] * 2,
        scratch_shapes=[
            vmem(128, 1024), vmem(128, 1024), vmem(1024, 1024), half(256, 1024), vmem(128, 1024),
            vmem(128, 1024), vmem(128, 1024), vmem(2, 1, 128), vmem(38, 1, 128), half(256, 1536), half(256, 1024),
            half(8, 2, 2, 2, 16, 1024),
            vmem(4, 64, WIN), vmem(4, 64, WIN), vmem(4, 2, 2, 4, 16, WIN),
            vmem(1024, 1024), half(1024, 1024), half(1024, 1024), half(1024, 1024),
            half(1024, 1024), vmem(1024, 1024), half(1024, 1024),
            half(4, 64, 1024), half(4, 64, 1024), half(4, 4, 2, 2, 16, 1024),
            bufs(vmem, WIN, (8, WIN)), bufs(half, 1024, (16, 512)),
            pltpu.SemaphoreType.DMA((3,)), pltpu.SemaphoreType.DMA((n_copies,)),
            pltpu.SemaphoreType.DMA((n_copies,)),
        ],
        compiler_params=pltpu.CompilerParams(
            collective_id=0, has_side_effects=True, vmem_limit_bytes=59000 * 1024),
        name="step",
    )(gradient, weight, dual)


def local(gradient, weight, dual):
    local_rows, col_count = gradient.shape[1:]
    threshold = 0.5 * math.sqrt(
        local_rows * lax.axis_size(ROW) * col_count * lax.axis_size("grp"))
    iterate, dual_next = step_of(gradient[0], weight[0], dual[0], threshold)
    update = math.sqrt(col_count) * iterate.astype(F32)
    return (update[None], dual_next[None])


def solution(mesh):
    torus = Mesh(
        mesh.devices.reshape(mesh.shape["grp"], 4, 4, 2), ("grp", "row_0", "row_1", "row_2")
    )
    in_specs = (P("grp", ROW, None), P("grp", ROW, None), P("grp", None, None))
    out_specs = (P("grp", ROW, None), P("grp", ROW, None))
    return jax.shard_map(local, mesh=torus, in_specs=in_specs, out_specs=out_specs, check_vma=False)
```

profile of v0, /device:TPU:1, one launch (start us, length us, event | category | flops | bytes accessed | tf_op | source)
XLA Modules:
  0.0 88.9 jit_solution(10140975622504554456)
XLA Ops:
  0.6 84.9 %step.1 = (bf16[128,1024]{1,0:T(8,128)(2,1)}, f32[32,1024]{1,0:T(8,128)}) custom-call(f32[128,1024]{1,0:T(8,128)} %bitcast.7, f32[128,1024]{1,0:T(8,128)} %bitcast.8, f32[1024,1024]{1,0:T(8,128)} %bitcast.6), custom_call_target="tpu_custom_call" | custom-call | tf_op jit(solution)/shard_map/step/pallas_call | solution.py:397
  85.5 1.8 %multiply_bitcast_fusion = f32[1,128,1024]{2,1,0:T(8,128)} fusion(bf16[128,1024]{1,0:T(8,128)(2,1)} %get-tuple-element.4), kind=kLoop, calls=%fused_computation | loop fusion | flops 262144 | bytes 786432 | tf_op jit(solution)/shard_map/broadcast_in_dim | solution.py:427
  87.3 1.6 %copy.6 = f32[1,32,1024]{2,1,0:T(8,128)} copy(f32[1,32,1024]{2,1,0:T(8,128)} %bitcast.9) | data formatting | bytes 262144
where the time goes:
time: 89 us; the launch traced here: 88.9 us
  Pallas kernels  84.9 us (95%)
  other arithmetic  1.8 us (2%)
  local copies, waits for them, and re-layouts  1.57 us (2%)
    pallas_call x1, Pallas kernels, step_of(): pl.pallas_call(lambda *refs: kernel(threshold, *refs), out_shape=(jax.Sha...  84.9 us
    broadcast_in_dim x1, other arithmetic, local(): return (update[None], dual_next[None])  1.8 us

commit v1 on v0

v1 whole, which is shorter than its diff:
```python
import math

import jax
import jax.numpy as jnp
from jax import lax
from jax.experimental import pallas as pl
from jax.experimental.pallas import tpu as pltpu
from jax.sharding import Mesh
from jax.sharding import PartitionSpec as P

ROW = ("row_0", "row_1", "row_2")
MESH = pl.DeviceIdType.MESH
coef_a = 3.4445
coef_b = -4.775
coef_c = 2.0315
epsilon = 1e-06
WIN = 640
STEPS = {8: (1,), 15: (1, 2), 22: (2,)}
F32 = jnp.float32
BF16 = jnp.bfloat16


class Copies:
    def __init__(self, send, recv):
        self.send, self.recv, self.n = send, recv, 0

    def __call__(self, src, dst, where):
        i = self.n
        self.n += 1
        copy = pltpu.make_async_remote_copy(
            src_ref=src, dst_ref=dst, send_sem=self.send.at[i], recv_sem=self.recv.at[i],
            device_id=where, device_id_type=MESH,
        )
        copy.start()
        return copy


def turn(p, d, n):
    return lax.rem(p + d, n)


class Sum:
    def __init__(self, copies, axis, p, part, arrived):
        self.p, self.part, self.arrived = p, part, arrived
        self.sent = [copies(part.at[turn(p, d, 4)], arrived.at[d - 1], {axis: turn(p, d, 4)})
                     for d in (2, 1, 3)]

    def total(self):
        for copy in self.sent:
            copy.wait_recv()
        out = self.part[self.p].astype(F32)
        for d in range(3):
            out += self.arrived[d].astype(F32)
        return out


class Spread:
    def __init__(self, copies, axis, p, at):
        self.sent = [copies(at(p), at(p), {axis: turn(p, d, 4)}) for d in (2, 1, 3)]
        self.came = [at(turn(p, 4 - d, 4)) for d in (2, 1, 3)]

    def each(self):
        for copy, ref in ((self.sent[i], self.came[i]) for i in (1, 2, 0)):
            copy.wait_recv()
            yield ref


def reduce_steps(c, x, y, parts_a, parts_b, bufs, put_a, put_b, sent):
    ra, rb, qa, qb, ra2, rb2 = bufs
    dtype = qa.dtype
    sum_a = Sum(c, "row_1", x, parts_a, ra)
    sum_b = Sum(c, "row_0", y, parts_b, rb)
    yield
    va = sum_a.total().astype(dtype)
    for j in range(4):
        qa[j] = va[16 * j:16 * j + 16]
    sum_a2 = Sum(c, "row_0", y, qa, ra2)
    vb = sum_b.total().astype(dtype)
    for j in range(4):
        qb[j] = vb[16 * j:16 * j + 16]
    sum_b2 = Sum(c, "row_1", x, qb, rb2)
    yield
    put_a(sum_a2.total())
    put_b(sum_b2.total())
    for phase in (sum_a, sum_b, sum_a2, sum_b2):
        sent += phase.sent


def gather_steps(c, x, y, k, near_at, far_at, sent):
    near_a, near_b = near_at
    far_a, far_b = far_at
    shared = []

    def pair(ref):
        shared.append(c(ref, ref, {"row_2": 1 - k}))

    na = Spread(c, "row_0", y, near_a)
    nb = Spread(c, "row_1", x, near_b)
    yield
    for _ in na.each():
        pass
    fa = Spread(c, "row_1", x, far_a)
    for _ in nb.each():
        pass
    fb = Spread(c, "row_0", y, far_b)
    pair(far_a(x))
    pair(far_b(y))
    yield
    for refs in zip(fa.each(), fb.each()):
        for ref in refs:
            pair(ref)
    yield
    for copy in shared:
        copy.wait_recv()
    for phase in (na, nb, fa, fb):
        sent += phase.sent
    sent += shared


def kernel(threshold, g_hbm, w_hbm, d_hbm, x_out, dual_out,
           g_ref, w_v, d_v, wst, wt, wt2, g2, stat_s, stat_r, xd, wd, cp, pa, pb, fin, fil, gf, gh, gl, p0, p1, p2, uf, ub,
           ca, cb, cfin, bufs_g, bufs_c, in_sem, send, recv):
    z = lax.axis_index("grp")
    y = lax.axis_index("row_0")
    x = lax.axis_index("row_1")
    k = lax.axis_index("row_2")
    other = 1 - k
    c = Copies(send, recv)
    load_d = pltpu.make_async_copy(d_hbm, d_v, in_sem.at[0])
    load_w = pltpu.make_async_copy(w_hbm, w_v, in_sem.at[1])
    load_g = pltpu.make_async_copy(g_hbm, g_ref, in_sem.at[2])
    load_g.start()
    load_w.start()
    load_d.start()

    barrier = pltpu.get_barrier_semaphore()
    partner = {"row_2": other}
    plane = [{"row_0": turn(y, e, 4), "row_1": turn(x, d, 4), "row_2": turn(k, f, 2)}
             for e in range(4) for d in range(4) for f in range(2) if (e, d, f) != (0, 0, 0)]
    line = [{"grp": turn(z, d, 8)} for d in range(1, 8)]
    for peer in plane + line:
        pl.semaphore_signal(barrier, inc=1, device_id=peer, device_id_type=MESH)

    load_g.wait()
    g = g_ref[...]
    total = jnp.full((1, 128), jnp.sum(g * g), F32)
    stat_s[0] = total
    own = pl.ds(pl.multiple_of(128 * k, 128), 128)
    theirs = pl.ds(pl.multiple_of(128 * other, 128), 128)
    pl.semaphore_wait(barrier, len(plane) + len(line))
    stats = [c(stat_s.at[0], stat_r.at[i], peer) for i, peer in enumerate(plane)]
    pairs = [c(g_ref, g2, partner)]
    load_w.wait()
    w = w_v[...]
    wh = w.astype(BF16)
    wst[0:128] = wh
    wst[128:256] = (w - wh.astype(F32)).astype(BF16)
    wd[own] = wh
    pairs.append(c(wd.at[own], wd.at[own], partner))
    load_d.wait()

    def split(v):
        vh = v.astype(BF16)
        return vh, (v - vh.astype(F32)).astype(BF16)

    def weighted_chunk(j):
        cols = pl.ds(256 * j, 256)
        dh, dl = split(d_v[:, cols])
        both = jnp.dot(wst[...], dh, preferred_element_type=F32)
        acc = both[:128] + both[128:] + jnp.dot(wst[0:128], dl, preferred_element_type=F32)
        dh, dl = split(d_v[cols, :])
        dims = (((1,), (1,)), ((), ()))
        both = lax.dot_general(wst[...], dh, dims, preferred_element_type=F32)
        acc += both[:128] + both[128:]
        acc += lax.dot_general(wst[0:128], dl, dims, preferred_element_type=F32)
        wt[:, cols] = 0.5 * acc

    def half_weighted(m):
        for n in (2 * m, 2 * m + 1):
            weighted_chunk(n)
        cols = pl.ds(512 * m, 512)
        pairs.append(c(wt.at[:, cols], wt2.at[:, cols], partner))

    half_weighted(0)
    for i, copy in enumerate(stats):
        copy.wait_recv()
        total += stat_r[i]
    stat_s[1] = total
    lines = [c(stat_s.at[1], stat_r.at[31 + i], peer) for i, peer in enumerate(line)]
    half_weighted(1)
    for copy in pairs:
        copy.wait_recv()
    for i, copy in enumerate(lines):
        copy.wait_recv()
        total += stat_r[31 + i]

    clip = jnp.minimum(1.0, threshold * lax.rsqrt(total[0:1, 0:1]))
    for rows, ga, wa in ((own, g_ref, wt), (theirs, g2, wt2)):
        t = (clip * ga[...] + wa[...]).astype(BF16)
        xd[rows, 0:1024] = t
        xd[rows, 1024:1536] = t[:, 0:512]

    tn = (((0,), (0,)), ((), ()))
    for i in range(4):
        at = pl.multiple_of(128 * (2 * i + k), 128)
        part = lax.dot_general(
            xd[:, pl.ds(at, 128)], xd[:, pl.ds(at, WIN)], tn, preferred_element_type=F32)
        pa[i] = part[:64]
        pb[i] = part[64:]

    ended = []

    def put_gram(at_hi, at_lo):
        def put(v):
            hi = v.astype(BF16)
            at_hi[...] = hi
            at_lo[...] = (v - hi.astype(F32)).astype(BF16)
        return put

    near = lambda f: (lambda j: f.at[x, k, 0, j], lambda j: f.at[y, k, 1, j])
    far = lambda f: (lambda i: f.at[i, k, 0], lambda i: f.at[i, k, 1])
    gram_steps = reduce_steps(c, x, y, pa, pb, bufs_g,
                              put_gram(near(fin)[0](y), near(fil)[0](y)),
                              put_gram(near(fin)[1](x), near(fil)[1](x)), ended)
    next(gram_steps)
    for b in range(8):
        part = lax.dot_general(
            wd[:, 128 * b:128 * b + 128], xd[:, 0:1024], tn, preferred_element_type=F32)
        cp[b] = part.astype(BF16).reshape(2, 2, 2, 16, 1024)
    for e in range(4):
        for d in range(4):
            ca[d, 16 * e:16 * e + 16] = cp[2 * e + d // 2, d % 2, k, 0]
            cb[e, 16 * d:16 * d + 16] = cp[2 * e + d // 2, d % 2, k, 1]
    for _ in gram_steps:
        pass
    high = gather_steps(c, x, y, k, near(fin), far(fin), ended)
    low = gather_steps(c, x, y, k, near(fil), far(fil), ended)
    next(high)
    next(low)
    next(high)
    next(low)

    def put_at(ref):
        def put(v):
            ref[...] = v.astype(BF16)
        return put

    product_near = (lambda j: cfin.at[j, x, k, 0], lambda j: cfin.at[y, j, k, 1])
    product_far = (lambda i: cfin.at[:, i, k, 0], lambda i: cfin.at[i, :, k, 1])
    reduced = reduce_steps(c, x, y, ca, cb, bufs_c, put_at(product_near[0](y)),
                           put_at(product_near[1](x)), ended)
    gathered = gather_steps(c, x, y, k, product_near, product_far, ended)
    next(reduced)
    for _ in high:
        pass

    trace = jnp.zeros((1, 1), F32)
    eye = (lax.broadcasted_iota(jnp.int32, (128, 128), 0)
           == lax.broadcasted_iota(jnp.int32, (128, 128), 1))
    for b in range(8):
        i, core = b // 2, b % 2
        for j in range(5):
            m = (b + j) % 8
            block = fin[i, core, :, :, :, 128 * j:128 * j + 128].reshape(128, 128)
            rows, cols = pl.ds(128 * b, 128), pl.ds(128 * m, 128)
            gh[rows, cols] = block
            if j == 0:
                trace += jnp.sum(jnp.where(eye, block.astype(F32), 0.0), keepdims=True)
            if 0 < j < 4:
                gh[cols, rows] = block.T
    scale = 1.0 / (trace + epsilon)
    root = jnp.sqrt(scale)

    def dot(u, v):
        return jnp.dot(u, v, preferred_element_type=F32)

    TILE = 256
    tiles = [pl.ds(TILE * n, TILE) for n in range(1024 // TILE)]
    done = [0]

    def advance():
        done[0] += 1
        for steps in STEPS.get(done[0], ()):
            next((low, reduced, gathered)[steps], None)

    def square(p, n, s):
        g = gh[:, n].astype(F32) if p is p0 else gf[:, n]
        p[:, n] = ((coef_b * s) * g + (coef_c * s * s) * dot(gh[...], gh[:, n])).astype(BF16)
        advance()

    def left(p, n):
        g = gh[:, n].astype(F32) if p is p0 else gf[:, n]
        u = coef_a * g + dot(p[...], gh[:, n])
        uf[:, n] = u
        ub[:, n] = u.astype(BF16)
        advance()

    def right(p, n, s):
        v = coef_a * uf[:, n] + dot(ub[...], p[:, n])
        if p is p0:
            v = s * (v + (coef_a * coef_a) * gl[:, n].astype(F32))
        gf[:, n] = v
        gh[:, n] = v.astype(BF16)
        advance()

    for n in tiles:
        square(p0, n, scale)
    for n in tiles:
        left(p0, n)
    for _ in low:
        pass
    for b in range(8):
        i, core = b // 2, b % 2
        for j in range(5):
            m = (b + j) % 8
            block = fil[i, core, :, :, :, 128 * j:128 * j + 128].reshape(128, 128)
            rows, cols = pl.ds(128 * b, 128), pl.ds(128 * m, 128)
            gl[rows, cols] = block
            if 0 < j < 4:
                gl[cols, rows] = block.T
    for n in tiles:
        right(p0, n, scale)
    for n in tiles:
        square(p1, n, 1.0)
    for n in tiles:
        left(p1, n)
    for n in tiles:
        right(p1, n, 1.0)
    for n in tiles:
        square(p2, n, 1.0)

    mine = cfin[y, x, k].reshape(32, 1024)
    share = 8 * y + 2 * x + k
    unit = (lax.broadcasted_iota(jnp.int32, (32, 1024), 0) + 32 * share
            == lax.broadcasted_iota(jnp.int32, (32, 1024), 1))
    stack = jnp.concatenate([xd[own, 0:1024], mine, unit.astype(F32).astype(BF16)], axis=0)
    v = coef_a * stack.astype(F32) + dot(stack, p0[...])
    v = coef_a * v + dot(v.astype(BF16), p1[...])
    v = coef_a * v + dot(v.astype(BF16), p2[...])

    def by_gram(v):
        v = dot((coef_a * v + dot(v.astype(BF16), p2[...])).astype(BF16), gh[...])
        return coef_a * v + dot(v.astype(BF16), p2[...])

    once = by_gram(v)
    next(gathered)
    v = coef_a * v + coef_b * once + coef_c * by_gram(once)
    for _ in gathered:
        pass
    x_out[...] = (root * v[0:128]).astype(BF16)
    cross = v[128:160] + lax.dot_general(
        v[160:192].astype(BF16), cfin[...].reshape(1024, 1024), (((1,), (1,)), ((), ())),
        preferred_element_type=F32)
    dual_out[...] = d_v[pl.ds(pl.multiple_of(32 * share, 32), 32), :] - (16.0 * root) * cross

    for copy in stats + lines + pairs + ended:
        copy.wait_send()


def step_of(gradient, weight, dual, threshold):
    vmem = lambda *s: pltpu.VMEM(s, F32)
    half = lambda *s: pltpu.VMEM(s, BF16)

    def bufs(kind, width):
        first, second = kind(3, 64, width), kind(3, 16, width)
        return [first, first, kind(4, 16, width), kind(4, 16, width), second, second]

    n_copies = 38 + 4 + 12 * 2 + 20 * 3
    return pl.pallas_call(
        lambda *refs: kernel(threshold, *refs),
        out_shape=(jax.ShapeDtypeStruct((128, 1024), BF16),
                   jax.ShapeDtypeStruct((32, 1024), F32)),
        in_specs=[pl.BlockSpec(memory_space=pltpu.HBM)] * 3,
        out_specs=[pl.BlockSpec(memory_space=pltpu.VMEM)] * 2,
        scratch_shapes=[
            vmem(128, 1024), vmem(128, 1024), vmem(1024, 1024), half(256, 1024), vmem(128, 1024),
            vmem(128, 1024), vmem(128, 1024), vmem(2, 1, 128), vmem(38, 1, 128), half(256, 1536), half(256, 1024),
            half(8, 2, 2, 2, 16, 1024),
            vmem(4, 64, WIN), vmem(4, 64, WIN), half(4, 2, 2, 4, 16, WIN), half(4, 2, 2, 4, 16, WIN),
            vmem(1024, 1024), half(1024, 1024), half(1024, 1024), half(1024, 1024), half(1024, 1024),
            half(1024, 1024), vmem(1024, 1024), half(1024, 1024),
            half(4, 64, 1024), half(4, 64, 1024), half(4, 4, 2, 2, 16, 1024),
            bufs(vmem, WIN), bufs(half, 1024),
            pltpu.SemaphoreType.DMA((3,)), pltpu.SemaphoreType.DMA((n_copies,)),
            pltpu.SemaphoreType.DMA((n_copies,)),
        ],
        compiler_params=pltpu.CompilerParams(
            collective_id=0, has_side_effects=True, vmem_limit_bytes=59000 * 1024),
        name="step",
    )(gradient, weight, dual)


def local(gradient, weight, dual):
    local_rows, col_count = gradient.shape[1:]
    threshold = 0.5 * math.sqrt(
        local_rows * lax.axis_size(ROW) * col_count * lax.axis_size("grp"))
    iterate, dual_next = step_of(gradient[0], weight[0], dual[0], threshold)
    update = math.sqrt(col_count) * iterate.astype(F32)
    return (update[None], dual_next[None])


def solution(mesh):
    torus = Mesh(
        mesh.devices.reshape(mesh.shape["grp"], 4, 4, 2), ("grp", "row_0", "row_1", "row_2")
    )
    in_specs = (P("grp", ROW, None), P("grp", ROW, None), P("grp", None, None))
    out_specs = (P("grp", ROW, None), P("grp", ROW, None))
    return jax.shard_map(local, mesh=torus, in_specs=in_specs, out_specs=out_specs, check_vma=False)
```

time: 89 us -> 80.9 us (0.909)
  Pallas kernels: 84.9 us -> 76.7 us
    pallas_call x1, Pallas kernels: 84.9 us -> 76.7 us  [step_of(): pl.pallas_call(lambda *refs: kernel(threshold, *refs), out_shape=(jax.Sha...]
where the time goes in v1:
time: 80.9 us; the launch traced here: 80.7 us
  Pallas kernels  76.7 us (95%)
  other arithmetic  1.8 us (2%)
  local copies, waits for them, and re-layouts  1.57 us (2%)
    pallas_call x1, Pallas kernels, step_of(): pl.pallas_call(lambda *refs: kernel(threshold, *refs), out_shape=(jax.Sha...  76.7 us
    broadcast_in_dim x1, other arithmetic, local(): return (update[None], dual_next[None])  1.8 us

profile of v1, /device:TPU:1, one launch (start us, length us, event | category | flops | bytes accessed | tf_op | source)
XLA Modules:
  0.0 80.7 jit_solution(8331954097403739211)
XLA Ops:
  0.6 76.7 %step.1 = (bf16[128,1024]{1,0:T(8,128)(2,1)}, f32[32,1024]{1,0:T(8,128)}) custom-call(f32[128,1024]{1,0:T(8,128)} %bitcast.7, f32[128,1024]{1,0:T(8,128)} %bitcast.8, f32[1024,1024]{1,0:T(8,128)} %bitcast.6), custom_call_target="tpu_custom_call" | custom-call | tf_op jit(solution)/shard_map/step/pallas_call | solution.py:369
  77.4 1.8 %multiply_bitcast_fusion = f32[1,128,1024]{2,1,0:T(8,128)} fusion(bf16[128,1024]{1,0:T(8,128)(2,1)} %get-tuple-element.4), kind=kLoop, calls=%fused_computation | loop fusion | flops 262144 | bytes 786432 | tf_op jit(solution)/shard_map/broadcast_in_dim | solution.py:399
  79.2 1.6 %copy.6 = f32[1,32,1024]{2,1,0:T(8,128)} copy(f32[1,32,1024]{2,1,0:T(8,128)} %bitcast.9) | data formatting | bytes 262144

commit v2 on v1

--- a/solution.py
+++ b/solution.py
@@ -15,7 +15,7 @@
 coef_c = 2.0315
 epsilon = 1e-06
 WIN = 640
-STEPS = {8: (1,), 15: (1, 2), 22: (2,)}
+STEPS = {1: (1, 2), 7: (2,), 21: (2,)}
 F32 = jnp.float32
 BF16 = jnp.bfloat16
 
@@ -231,6 +231,19 @@
         for d in range(4):
             ca[d, 16 * e:16 * e + 16] = cp[2 * e + d // 2, d % 2, k, 0]
             cb[e, 16 * d:16 * d + 16] = cp[2 * e + d // 2, d % 2, k, 1]
+    next(gram_steps)
+
+    def put_at(ref):
+        def put(v):
+            ref[...] = v.astype(BF16)
+        return put
+
+    product_near = (lambda j: cfin.at[j, x, k, 0], lambda j: cfin.at[y, j, k, 1])
+    product_far = (lambda i: cfin.at[:, i, k, 0], lambda i: cfin.at[i, :, k, 1])
+    reduced = reduce_steps(c, x, y, ca, cb, bufs_c, put_at(product_near[0](y)),
+                           put_at(product_near[1](x)), ended)
+    gathered = gather_steps(c, x, y, k, product_near, product_far, ended)
+    next(reduced)
     for _ in gram_steps:
         pass
     high = gather_steps(c, x, y, k, near(fin), far(fin), ended)
@@ -239,17 +252,6 @@
     next(low)
     next(high)
     next(low)
-
-    def put_at(ref):
-        def put(v):
-            ref[...] = v.astype(BF16)
-        return put
-
-    product_near = (lambda j: cfin.at[j, x, k, 0], lambda j: cfin.at[y, j, k, 1])
-    product_far = (lambda i: cfin.at[:, i, k, 0], lambda i: cfin.at[i, :, k, 1])
-    reduced = reduce_steps(c, x, y, ca, cb, bufs_c, put_at(product_near[0](y)),
-                           put_at(product_near[1](x)), ended)
-    gathered = gather_steps(c, x, y, k, product_near, product_far, ended)
     next(reduced)
     for _ in high:
         pass
@@ -343,7 +345,6 @@
         return coef_a * v + dot(v.astype(BF16), p2[...])
 
     once = by_gram(v)
-    next(gathered)
     v = coef_a * v + coef_b * once + coef_c * by_gram(once)
     for _ in gathered:
         pass

time: 80.9 us -> 81.6 us (level)
  no operation moved by 1% of the time
where the time goes in v2:
time: 81.6 us; the launch traced here: 81.5 us
  Pallas kernels  77.5 us (95%)
  other arithmetic  1.8 us (2%)
  local copies, waits for them, and re-layouts  1.57 us (2%)
    pallas_call x1, Pallas kernels, step_of(): pl.pallas_call(lambda *refs: kernel(threshold, *refs), out_shape=(jax.Sha...  77.5 us
    broadcast_in_dim x1, other arithmetic, local(): return (update[None], dual_next[None])  1.8 us

profile of v2, /device:TPU:1, one launch (start us, length us, event | category | flops | bytes accessed | tf_op | source)
XLA Modules:
  0.0 81.5 jit_solution(6496055870335355576)
XLA Ops:
  0.6 77.5 %step.1 = (bf16[128,1024]{1,0:T(8,128)(2,1)}, f32[32,1024]{1,0:T(8,128)}) custom-call(f32[128,1024]{1,0:T(8,128)} %bitcast.7, f32[128,1024]{1,0:T(8,128)} %bitcast.8, f32[1024,1024]{1,0:T(8,128)} %bitcast.6), custom_call_target="tpu_custom_call" | custom-call | tf_op jit(solution)/shard_map/step/pallas_call | solution.py:370
  78.1 1.8 %multiply_bitcast_fusion = f32[1,128,1024]{2,1,0:T(8,128)} fusion(bf16[128,1024]{1,0:T(8,128)(2,1)} %get-tuple-element.4), kind=kLoop, calls=%fused_computation | loop fusion | flops 262144 | bytes 786432 | tf_op jit(solution)/shard_map/broadcast_in_dim | solution.py:400
  79.9 1.6 %copy.6 = f32[1,32,1024]{2,1,0:T(8,128)} copy(f32[1,32,1024]{2,1,0:T(8,128)} %bitcast.9) | data formatting | bytes 262144

commit v3 on v2

--- a/solution.py
+++ b/solution.py
@@ -15,7 +15,7 @@
 coef_c = 2.0315
 epsilon = 1e-06
 WIN = 640
-STEPS = {1: (1, 2), 7: (2,), 21: (2,)}
+STEPS = {3: (1, 2), 4: (0,), 13: (2,)}
 F32 = jnp.float32
 BF16 = jnp.bfloat16
 
@@ -40,10 +40,17 @@
 
 
 class Sum:
-    def __init__(self, copies, axis, p, part, arrived):
+    def __init__(self, copies, axis, p, part, arrived, dist=(2, 1, 3)):
+        self.copies, self.axis = copies, axis
         self.p, self.part, self.arrived = p, part, arrived
-        self.sent = [copies(part.at[turn(p, d, 4)], arrived.at[d - 1], {axis: turn(p, d, 4)})
-                     for d in (2, 1, 3)]
+        self.sent = []
+        self.send(dist)
+
+    def send(self, dist):
+        for d in dist:
+            to = turn(self.p, d, 4)
+            self.sent.append(
+                self.copies(self.part.at[to], self.arrived.at[d - 1], {self.axis: to}))
 
     def total(self):
         for copy in self.sent:
@@ -65,12 +72,17 @@
             yield ref
 
 
-def reduce_steps(c, x, y, parts_a, parts_b, bufs, put_a, put_b, sent):
+def reduce_steps(c, x, y, parts_a, parts_b, bufs, put_a, put_b, sent, split=False):
     ra, rb, qa, qb, ra2, rb2 = bufs
     dtype = qa.dtype
-    sum_a = Sum(c, "row_1", x, parts_a, ra)
-    sum_b = Sum(c, "row_0", y, parts_b, rb)
+    first = (2,) if split else (2, 1, 3)
+    sum_a = Sum(c, "row_1", x, parts_a, ra, first)
+    sum_b = Sum(c, "row_0", y, parts_b, rb, first)
     yield
+    if split:
+        sum_a.send((1, 3))
+        sum_b.send((1, 3))
+        yield
     va = sum_a.total().astype(dtype)
     for j in range(4):
         qa[j] = va[16 * j:16 * j + 16]
@@ -241,7 +253,7 @@
     product_near = (lambda j: cfin.at[j, x, k, 0], lambda j: cfin.at[y, j, k, 1])
     product_far = (lambda i: cfin.at[:, i, k, 0], lambda i: cfin.at[i, :, k, 1])
     reduced = reduce_steps(c, x, y, ca, cb, bufs_c, put_at(product_near[0](y)),
-                           put_at(product_near[1](x)), ended)
+                           put_at(product_near[1](x)), ended, True)
     gathered = gather_steps(c, x, y, k, product_near, product_far, ended)
     next(reduced)
     for _ in gram_steps:
@@ -250,6 +262,7 @@
     low = gather_steps(c, x, y, k, near(fil), far(fil), ended)
     next(high)
     next(low)
+    next(reduced)
     next(high)
     next(low)
     next(reduced)
@@ -344,6 +357,7 @@
         v = dot((coef_a * v + dot(v.astype(BF16), p2[...])).astype(BF16), gh[...])
         return coef_a * v + dot(v.astype(BF16), p2[...])
 
+    next(gathered)
     once = by_gram(v)
     v = coef_a * v + coef_b * once + coef_c * by_gram(once)
     for _ in gathered:

time: 81.6 us -> 79 us (0.968)
  Pallas kernels: 77.5 us -> 74.9 us
    pallas_call x1, Pallas kernels: 77.5 us -> 74.9 us  [step_of(): pl.pallas_call(lambda *refs: kernel(threshold, *refs), out_shape=(jax.Sha...]
where the time goes in v3:
time: 79 us; the launch traced here: 78.9 us
  Pallas kernels  74.9 us (95%)
  other arithmetic  1.8 us (2%)
  local copies, waits for them, and re-layouts  1.57 us (2%)
    pallas_call x1, Pallas kernels, step_of(): pl.pallas_call(lambda *refs: kernel(threshold, *refs), out_shape=(jax.Sha...  74.9 us
    broadcast_in_dim x1, other arithmetic, local(): return (update[None], dual_next[None])  1.8 us

profile of v3, /device:TPU:1, one launch (start us, length us, event | category | flops | bytes accessed | tf_op | source)
XLA Modules:
  0.0 78.9 jit_solution(15184277900943954129)
XLA Ops:
  0.6 74.9 %step.1 = (bf16[128,1024]{1,0:T(8,128)(2,1)}, f32[32,1024]{1,0:T(8,128)}) custom-call(f32[128,1024]{1,0:T(8,128)} %bitcast.7, f32[128,1024]{1,0:T(8,128)} %bitcast.8, f32[1024,1024]{1,0:T(8,128)} %bitcast.6), custom_call_target="tpu_custom_call" | custom-call | tf_op jit(solution)/shard_map/step/pallas_call | solution.py:384
  75.5 1.8 %multiply_bitcast_fusion = f32[1,128,1024]{2,1,0:T(8,128)} fusion(bf16[128,1024]{1,0:T(8,128)(2,1)} %get-tuple-element.4), kind=kLoop, calls=%fused_computation | loop fusion | flops 262144 | bytes 786432 | tf_op jit(solution)/shard_map/broadcast_in_dim | solution.py:414
  77.3 1.6 %copy.6 = f32[1,32,1024]{2,1,0:T(8,128)} copy(f32[1,32,1024]{2,1,0:T(8,128)} %bitcast.9) | data formatting | bytes 262144

commit v4 on v3

--- a/solution.py
+++ b/solution.py
@@ -1,3 +1,4 @@
+import functools
 import math
 
 import jax
@@ -15,7 +16,7 @@
 coef_c = 2.0315
 epsilon = 1e-06
 WIN = 640
-STEPS = {3: (1, 2), 4: (0,), 13: (2,)}
+STEPS = {4: (0,), 8: (1,), 16: (1, 2), 23: (2,)}
 F32 = jnp.float32
 BF16 = jnp.bfloat16
 
@@ -255,16 +256,15 @@
     reduced = reduce_steps(c, x, y, ca, cb, bufs_c, put_at(product_near[0](y)),
                            put_at(product_near[1](x)), ended, True)
     gathered = gather_steps(c, x, y, k, product_near, product_far, ended)
-    next(reduced)
     for _ in gram_steps:
         pass
     high = gather_steps(c, x, y, k, near(fin), far(fin), ended)
     low = gather_steps(c, x, y, k, near(fil), far(fil), ended)
     next(high)
     next(low)
-    next(reduced)
     next(high)
     next(low)
+    next(reduced)
     next(reduced)
     for _ in high:
         pass
@@ -405,12 +405,22 @@
     )(gradient, weight, dual)
 
 
+def finish(width_root, x_ref, d_ref, update_ref, dual_ref):
+    update_ref[...] = width_root * x_ref[...].astype(F32)
+    dual_ref[...] = d_ref[...]
+
+
 def local(gradient, weight, dual):
     local_rows, col_count = gradient.shape[1:]
     threshold = 0.5 * math.sqrt(
         local_rows * lax.axis_size(ROW) * col_count * lax.axis_size("grp"))
     iterate, dual_next = step_of(gradient[0], weight[0], dual[0], threshold)
-    update = math.sqrt(col_count) * iterate.astype(F32)
+    update, dual_next = pl.pallas_call(
+        functools.partial(finish, math.sqrt(col_count)),
+        out_shape=(jax.ShapeDtypeStruct((local_rows, col_count), F32),
+                   jax.ShapeDtypeStruct(dual_next.shape, F32)),
+        name="finish",
+    )(iterate, dual_next)
     return (update[None], dual_next[None])
 
 

time: 79 us -> 77.2 us (0.977)
  other arithmetic: 1.8 us -> 0 us
  Pallas kernels: 74.9 us -> 76.5 us
  local copies, waits for them, and re-layouts: 1.57 us -> 0 us
    pallas_call x0 -> x1, Pallas kernels: none -> 1.85 us  [local(): pl.pallas_call(functools.partial(finish, math.sqrt(col_count)), out_shape...]
    broadcast_in_dim x1 -> x0, other arithmetic: 1.8 us -> none  [local(): return (update[None], dual_next[None])]
    unnamed x1 -> x0, local copies, waits for them, and re-layouts: 1.57 us -> none
where the time goes in v4:
time: 77.2 us; the launch traced here: 77.1 us
  Pallas kernels  76.5 us (99%)
    pallas_call x1, Pallas kernels, step_of(): pl.pallas_call(lambda *refs: kernel(threshold, *refs), out_shape=(jax.Sha...  74.6 us
    pallas_call x1, Pallas kernels, local(): pl.pallas_call(functools.partial(finish, math.sqrt(col_count)), out_shape...  1.85 us

profile of v4, /device:TPU:1, one launch (start us, length us, event | category | flops | bytes accessed | tf_op | source)
XLA Modules:
  0.0 77.1 jit_solution(6573364386818365913)
XLA Ops:
  0.6 74.6 %step.1 = (bf16[128,1024]{1,0:T(8,128)(2,1)}, f32[32,1024]{1,0:T(8,128)}) custom-call(f32[128,1024]{1,0:T(8,128)} %bitcast.6, f32[128,1024]{1,0:T(8,128)} %bitcast.7, f32[1024,1024]{1,0:T(8,128)} %bitcast.5), custom_call_target="tpu_custom_call" | custom-call | tf_op jit(solution)/shard_map/step/pallas_call | solution.py:384
  75.3 1.9 %finish.1 = (f32[128,1024]{1,0:T(8,128)}, f32[32,1024]{1,0:T(8,128)}) custom-call(bf16[128,1024]{1,0:T(8,128)(2,1)} %get-tuple-element.6.x_ref, f32[32,1024]{1,0:T(8,128)} %get-tuple-element.7.d_ref), custom_call_target="tpu_custom_call" | custom-call | tf_op jit(solution)/shard_map/finish/pallas_call | solution.py:418

commit v5 on v4

--- a/solution.py
+++ b/solution.py
@@ -298,9 +298,16 @@
         for steps in STEPS.get(done[0], ()):
             next((low, reduced, gathered)[steps], None)
 
-    def square(p, n, s):
-        g = gh[:, n].astype(F32) if p is p0 else gf[:, n]
-        p[:, n] = ((coef_b * s) * g + (coef_c * s * s) * dot(gh[...], gh[:, n])).astype(BF16)
+    def mirror(ref, t, v):
+        for m in range(1, v.shape[0] // TILE):
+            ref[tiles[t], pl.ds(TILE * (t + m), TILE)] = v[TILE * m:TILE * m + TILE].T
+
+    def square(p, t, s):
+        rows, n = pl.ds(TILE * t, 1024 - TILE * t), tiles[t]
+        g = gh[rows, n].astype(F32) if p is p0 else gf[rows, n]
+        v = ((coef_b * s) * g + (coef_c * s * s) * dot(gh[rows, :], gh[:, n])).astype(BF16)
+        p[rows, n] = v
+        mirror(p, t, v)
         advance()
 
     def left(p, n):
@@ -318,8 +325,8 @@
         gh[:, n] = v.astype(BF16)
         advance()
 
-    for n in tiles:
-        square(p0, n, scale)
+    for t in range(len(tiles)):
+        square(p0, t, scale)
     for n in tiles:
         left(p0, n)
     for _ in low:
@@ -335,14 +342,19 @@
                 gl[cols, rows] = block.T
     for n in tiles:
         right(p0, n, scale)
-    for n in tiles:
-        square(p1, n, 1.0)
+    for t in range(len(tiles)):
+        square(p1, t, 1.0)
     for n in tiles:
         left(p1, n)
-    for n in tiles:
-        right(p1, n, 1.0)
-    for n in tiles:
-        square(p2, n, 1.0)
+    for t in range(len(tiles)):
+        rows, n = pl.ds(TILE * t, 1024 - TILE * t), tiles[t]
+        v = coef_a * uf[rows, n] + dot(ub[rows, :], p1[:, n])
+        gf[rows, n] = v
+        gh[rows, n] = v.astype(BF16)
+        mirror(gh, t, v.astype(BF16))
+        advance()
+    for t in range(len(tiles)):
+        square(p2, t, 1.0)
 
     mine = cfin[y, x, k].reshape(32, 1024)
     share = 8 * y + 2 * x + k

time: 77.2 us -> 74.7 us (0.968)
  Pallas kernels: 76.5 us -> 74 us
    pallas_call x1, Pallas kernels: 74.6 us -> 72.1 us  [step_of(): pl.pallas_call(lambda *refs: kernel(threshold, *refs), out_shape=(jax.Sha...]
where the time goes in v5:
time: 74.7 us; the launch traced here: 74.6 us
  Pallas kernels  74 us (99%)
    pallas_call x1, Pallas kernels, step_of(): pl.pallas_call(lambda *refs: kernel(threshold, *refs), out_shape=(jax.Sha...  72.1 us
    pallas_call x1, Pallas kernels, local(): pl.pallas_call(functools.partial(finish, math.sqrt(col_count)), out_shape...  1.85 us

profile of v5, /device:TPU:1, one launch (start us, length us, event | category | flops | bytes accessed | tf_op | source)
XLA Modules:
  0.0 74.6 jit_solution(1891158454960155921)
XLA Ops:
  0.6 72.1 %step.1 = (bf16[128,1024]{1,0:T(8,128)(2,1)}, f32[32,1024]{1,0:T(8,128)}) custom-call(f32[128,1024]{1,0:T(8,128)} %bitcast.6, f32[128,1024]{1,0:T(8,128)} %bitcast.7, f32[1024,1024]{1,0:T(8,128)} %bitcast.5), custom_call_target="tpu_custom_call" | custom-call | tf_op jit(solution)/shard_map/step/pallas_call | solution.py:396
  72.8 1.9 %finish.1 = (f32[128,1024]{1,0:T(8,128)}, f32[32,1024]{1,0:T(8,128)}) custom-call(bf16[128,1024]{1,0:T(8,128)(2,1)} %get-tuple-element.6.x_ref, f32[32,1024]{1,0:T(8,128)} %get-tuple-element.7.d_ref), custom_call_target="tpu_custom_call" | custom-call | tf_op jit(solution)/shard_map/finish/pallas_call | solution.py:430
